TPU v7x, 256 devices: a whole 4x4x8 slice. The times are simulated.
256 devices in a mesh: obs: 64 (over z, x, core), sub: 4 (over y).
Axes of the slice: x: 4, y: 4, z: 8, core: 2. Of those that a mesh axis runs over, the one named last changes fastest.
Arguments:
- jacobian: bfloat16 [262144, 2048], P(('obs', 'sub')), may hold values from -0.09375 to 0.09375
- obs_weight: float32 [262144], P(('obs', 'sub')), may hold values from 0.2 to 5
- row_counts: int32 [64], P('obs'), may hold values from 1 to 4096, 196608 in all
- tile_lists: int32 [64, 8], replicated, may hold values from 0 to 15, all different within a row
- tile_slot: int32 [16], replicated, may hold values from 0 to 15, each once
- probe_block: bfloat16 [4096, 256], P('obs'), may hold values from -6 to 6
Outputs:
- owned_product: bfloat16 [4096, 256], P('obs', 'sub')
Inputs may be any that keep to these rules, and one draw needn't show every extreme that they name: `row_counts`: the live counts of one block; some block is full (4096) in every draw. `tile_lists`: each row lists 8 different tiles; every tile is listed by some block. `tile_slot`: a permutation of the tiles.
All inputs are finite; a program needn't handle non-finite values.
Results may differ from a plain program's by a relative error of at most 0.0034.
Values may be sent and summed in bfloat16 or wider, within the bound.
A program may use at most 64 MiB of HBM per device.

v0:
```python
import jax
import jax.numpy as jnp
from jax import lax
from jax.sharding import PartitionSpec as P


def local(jacobian, obs_weight, row_counts, tile_lists, tile_slot, probe_block):
    rows = jacobian.shape[0]
    width = jacobian.shape[1]
    tiles_listed = tile_lists.shape[1]
    tile_count = tile_slot.shape[0]
    tile_rows = width // tiles_listed
    obs_count = lax.axis_size("obs")
    own_rows = tile_count * tile_rows // obs_count
    block_id = lax.axis_index("obs")
    sub_id = lax.axis_index("sub")
    offset = sub_id * rows
    live = (offset + jnp.arange(rows, dtype=jnp.int32) < row_counts[0]).astype(jnp.float32)
    weighted = (jacobian.astype(jnp.float32) * (obs_weight * live)[:, None]).astype(jnp.bfloat16)
    my_tiles = lax.dynamic_slice_in_dim(tile_lists, block_id, 1, 0)[0]
    contract_rows = (((0,), (0,)), ((), ()))
    within = jnp.arange(tile_rows, dtype=jnp.int32)
    wanted_rows = (my_tiles[:, None] * tile_rows + within[None, :]).reshape(width)
    piece = lax.all_gather(probe_block, "obs", axis=0, tiled=True)
    global_rows = jnp.arange(piece.shape[0], dtype=jnp.int32)
    selector = (wanted_rows[:, None] == global_rows[None, :]).astype(jnp.bfloat16)
    probe_cols = jnp.dot(selector, piece, preferred_element_type=jnp.float32).astype(jnp.bfloat16)
    image = jnp.dot(jacobian, probe_cols, preferred_element_type=jnp.float32).astype(jnp.bfloat16)
    partial_prod = lax.dot_general(
        weighted, image, contract_rows, preferred_element_type=jnp.float32
    )
    tile_ids = jnp.arange(tile_count, dtype=jnp.int32)
    slots = jnp.sum(
        (my_tiles[:, None] == tile_ids[None, :]).astype(jnp.int32) * tile_slot[None, :], axis=1
    )
    positions = jnp.arange(tiles_listed, dtype=jnp.int32)
    block_sum = lax.psum_scatter(partial_prod, "sub", scatter_dimension=1, tiled=True)
    targets = jnp.arange(own_rows * lax.axis_size("obs"), dtype=jnp.int32)
    target_slot = targets // tile_rows
    match = (slots[None, :] == target_slot[:, None]).astype(jnp.int32)
    found = jnp.sum(match, axis=1)
    where_at = jnp.sum(match * positions[None, :], axis=1)
    source_rows = where_at * tile_rows + targets % tile_rows
    taken = jnp.take(block_sum, source_rows, axis=0)
    summed = lax.psum_scatter(
        taken * found[:, None].astype(jnp.float32), "obs", scatter_dimension=0, tiled=True
    )
    return summed.astype(jnp.bfloat16)


def solution(mesh):
    placed = (P(("obs", "sub"), None), P(("obs", "sub")), P("obs"), P(), P(), P("obs", None))
    return jax.shard_map(
        local, mesh=mesh, in_specs=placed, out_specs=P("obs", "sub"), check_vma=False
    )
```

profile of v0, /device:TPU:8, one launch (start us, length us, event | category | flops | bytes accessed | tf_op | source)
XLA Modules:
  0.0 300.9 jit_solution(16359943806372789093)
XLA Ops:
  6.5 0.0 copy-start
  6.5 0.0 all-gather.2.cloned.1.call-start
  6.5 0.7 all-gather.2.cloned.1.call-update
  7.3 0.0 reduce-scatter.3.cloned.1.call-start
  8.0 0.0 copy-done
  8.0 0.2 dynamic-slice_reduce_fusion
  8.2 0.1 add_bitcast_fusion
  8.2 0.7 fusion.18
  8.9 81.4 %all-gather.2.cloned.1.call-done = bf16[4096,256]{1,0:T(8,128)(2,1)} async-done(((bf16[64,256]{1,0:T(8,128)(2,1)}), bf16[4096,256]{1,0:T(8,128)(2,1)}) %all-gather.2.cloned.1.call-update) | async-done | bytes 2097168 | tf_op jit(solution)/shard_map/all_gather | solution.py:24
  90.3 11.4 %fusion.6 = bf16[256,1024]{1,0:T(8,128)(2,1)S(1)} fusion(bf16[1024,2048]{1,0:T(8,128)(2,1)} %param.6, bf16[4096,256]{1,0:T(8,128)(2,1)} %all-gather.2.cloned.1.call-done, s32[2048]{0:T(1024)S(1)} %bitcast.12), kind=kOutput, calls=%fused_computation.10 | convolution fusion | flops 5377884160 | bytes 6823936 | tf_op jit(solution)/shard_map/dot_general | solution.py:28
  101.7 4.9 %fusion.2 = f32[2048,256]{0,1:T(8,128)} fusion(bf16[256,1024]{1,0:T(8,128)(2,1)S(1)} %fusion.6, bf16[1024,2048]{1,0:T(8,128)(2,1)} %param.6, f32[1024]{0:T(1024)S(1)} %fusion.18), kind=kOutput, calls=%fused_computation.5 | convolution fusion | flops 1080033280 | bytes 6819840 | tf_op jit(solution)/shard_map/dot_general | solution.py:29
  106.6 0.0 copy-start.1
  106.6 0.0 reduce-scatter.3.cloned.1.call-update
  106.7 0.0 reduce-scatter.5.cloned.1.call-start
  106.7 0.6 copy-done.1
  107.3 0.2 select_reduce_fusion
  107.5 0.1 fusion.8
  107.7 27.8 %reduce-scatter.3.cloned.1.call-done = f32[2048,64]{0,1:T(8,128)} async-done(((f32[2048,256]{0,1:T(8,128)}), f32[2048,64]{0,1:T(8,128)}) %reduce-scatter.3.cloned.1.call-update) | async-done | bytes 524304 | tf_op jit(solution)/shard_map/reduce_scatter | solution.py:37
  135.5 1.4 copy.9
  136.9 10.8 %gather_fusion = f32[4096,64]{1,0:T(8,128)S(1)} fusion(f32[2048,64]{1,0:T(8,128)S(1)} %copy.9, s32[4096]{0:T(1024)S(1)} %broadcast_clamp_fusion), kind=kCustom, calls=%fused_computation | custom fusion | bytes 2113536 | tf_op jit(solution)/shard_map/jit(_take)/gather | solution.py:44
  147.6 2.7 select_multiply_fusion
  150.3 0.0 reduce-scatter.5.cloned.1.call-update
  150.3 142.7 %reduce-scatter.5.cloned.1.call-done = f32[64,64]{1,0:T(8,128)} async-done(((f32[4096,64]{1,0:T(8,128)}), f32[64,64]{1,0:T(8,128)}) %reduce-scatter.5.cloned.1.call-update) | async-done | bytes 16400 | tf_op jit(solution)/shard_map/reduce_scatter | solution.py:45
  293.0 1.4 convert_element_type.36
  (8 shorter events, 0.1 us)
Async XLA Ops:
  6.5 1.4 copy-start
  6.5 83.8 %all-gather.2.cloned.1.call-start = ((), (), s32[]{:S(2)}) async-start(), calls=%async_computation.2 | async-start | bytes 2129920 | tf_op jit(solution)/shard_map/all_gather | solution.py:24
  7.3 128.2 %reduce-scatter.3.cloned.1.call-start = ((), (), s32[]{:S(2)}) async-start(), calls=%async_computation.3 | async-start | bytes 2621440 | tf_op jit(solution)/shard_map/reduce_scatter | solution.py:37
  106.6 0.7 copy-start.1
  106.7 186.4 %reduce-scatter.5.cloned.1.call-start = ((), (), s32[]{:S(2)}) async-start(), calls=%async_computation.4 | async-start | bytes 2129920 | tf_op jit(solution)/shard_map/reduce_scatter | solution.py:45
Sparse Core Ops, SparseCore 0:
  10.1 80.1 all-gather.1
  106.8 28.6 reduce-scatter.2
  150.4 142.5 reduce-scatter.4
where the time goes:
time: 301 us
  waiting for transfers between devices  253 us (84%)
  matrix products  16.3 us (5%)
  between operations  13.8 us (5%)
  local copies, waits for them, and re-layouts  12.9 us (4%)
  other arithmetic  5.19 us (2%)
    reduce_scatter x1, waiting for transfers between devices, local(): lax.psum_scatter(taken * found[:, None].astype(jnp.float32), 'obs', scatt...  143 us
    all_gather x1, waiting for transfers between devices, local(): piece = lax.all_gather(probe_block, 'obs', axis=0, tiled=True)  81.4 us
    reduce_scatter x1, waiting for transfers between devices, local(): lax.psum_scatter(partial_prod, 'sub', scatter_dimension=1, tiled=True)  27.8 us
    dot_general x1, matrix products, local(): jnp.dot(jacobian, probe_cols, preferred_element_type=jnp.float32)  11.4 us
    gather x1, local copies, waits for them, and re-layouts, local(): taken = jnp.take(block_sum, source_rows, axis=0)  10.8 us
  transfers between devices with their start and end apart: 3, of which 3 were waited for; matrix products, arithmetic and copies ran while one was open for 0% of the time, Pallas kernels for 0%

commit v1 on v0

v1 whole, which is shorter than its diff:
```python
import jax
import jax.numpy as jnp
from jax import lax
from jax.experimental import pallas as pl
from jax.experimental.pallas import tpu as pltpu
from jax.sharding import PartitionSpec as P

MESH = pl.DeviceIdType.MESH
X, Y, Z = 4, 4, 8
F32, BF16 = jnp.float32, jnp.bfloat16

STAGES = 3


def kernel(lists_ref, slot_ref, count_ref, w_ref, jac_ref, probe_ref, out_ref,
           table, pb, jv, g, img, cown, csend, crecv, d, ra, rb, rc, e, r3, fin,
           s_loc, s_jac, s_a, r_a, s_b, r_b, s_ring, r_ring, s_p, r_p, s_c, r_c,
           s_q, r_q, s_z, r_z):
    obs, y = lax.axis_index("obs"), lax.axis_index("sub")
    c = obs % 2
    x = (obs // 2) % X
    z = obs // (2 * X)

    def dev(zz, xx, cc, yy=None):
        return ((zz * X + xx) * 2 + cc, y if yy is None else yy)

    def send(src, dst, s, r, to):
        copy = pltpu.make_async_remote_copy(src_ref=src, dst_ref=dst, send_sem=s, recv_sem=r, device_id=to, device_id_type=MESH)
        copy.start()
        return copy

    def arrived(dst, r):
        pltpu.make_async_remote_copy(src_ref=dst, dst_ref=dst, send_sem=s_loc.at[2], recv_sem=r, device_id=dev(z, x, 1 - c),
                                     device_id_type=MESH).wait_recv()

    def sent(src, s):
        pltpu.make_async_remote_copy(src_ref=src, dst_ref=src, send_sem=s, recv_sem=s_loc.at[2], device_id=dev(z, x, 1 - c),
                                     device_id_type=MESH).wait_send()

    partner = dev(z, x, 1 - c)
    pltpu.make_async_copy(probe_ref, pb, s_loc.at[0]).start()
    for k in range(8):
        pltpu.make_async_copy(jac_ref.at[:, pl.ds(k * 256, 256)], jv.at[k], s_jac.at[k]).start()

    barrier = pltpu.get_barrier_semaphore()
    others = [(z, (x + dx) % X, cc, y) for dx in range(1, X) for cc in range(2)]
    others += [((z + dz) % Z, x, cc, y) for dz in range(1, Z) for cc in range(2)]
    others += [(z, x, 1 - c, y), (z, x, c, (y + 1) % Y), (z, x, c, (y + Y - 1) % Y)]
    for o in others:
        pl.semaphore_signal(barrier, inc=1, device_id=dev(*o), device_id_type=MESH)

    def fill(t, _):
        for which, owner in enumerate((obs, obs + 1 - 2 * c)):
            at, found = jnp.int32(0), jnp.int32(0)
            for k in range(8):
                hit = slot_ref[lists_ref[k, owner]] == t
                at = jnp.where(hit, k, at)
                found = jnp.where(hit, 1, found)
            table[2 * which, t] = at
            table[2 * which + 1, t] = found
        return 0

    lax.fori_loop(0, 16, fill, 0)
    pltpu.make_async_copy(probe_ref, pb, s_loc.at[0]).wait()
    pl.semaphore_wait(barrier, len(others))

    half0, half1 = pb.at[:, pl.ds(0, 128)], pb.at[:, pl.ds(128, 128)]
    mine0 = g.at[0, z, x, pl.ds(c * 64, 64)]
    mine1 = g.at[1, z, x, pl.ds(c * 64, 64)]

    @pl.when(c == 0)
    def _():
        pltpu.make_async_copy(half0, mine0, s_loc.at[1]).start()
        send(half1, mine1, s_b.at[0], r_b.at[z * 2], partner)

    @pl.when(c == 1)
    def _():
        send(half0, mine0, s_a.at[0], r_a.at[x * 2 + 1], partner)
        pltpu.make_async_copy(half1, mine1, s_loc.at[1]).start()

    for dx in (1, 3, 2):
        send(half0, mine0, s_a.at[dx], r_a.at[x * 2 + c], dev(z, (x + dx) % X, 0))
    for dz in (4, 3, 5, 2, 6, 1, 7):
        send(half1, mine1, s_b.at[dz], r_b.at[z * 2 + c], dev((z + dz) % Z, x, 1))

    def piece0(zz, xx):
        return g.at[0, zz, xx]

    @pl.when(c == 0)
    def _():
        n = 0
        for i, dx in enumerate((0, 1, 3, 2)):
            xx = (x + dx) % X
            for cc in range(2):
                if dx == 0 and cc == 0:
                    pltpu.make_async_copy(half0, mine0, s_loc.at[1]).wait()
                else:
                    arrived(g.at[0, z, xx, pl.ds(cc * 64, 64)], r_a.at[xx * 2 + cc])
            for way, to in ((0, (z + 1) % Z), (1, (z + Z - 1) % Z)):
                send(piece0(z, xx), piece0(z, xx), s_ring.at[way, i], r_ring.at[way, i], dev(to, x, 0))
            send(piece0(z, xx), piece0(z, xx), s_p.at[n], r_p.at[n], partner)
            n += 1
        for step in range(1, 5):
            for i, dx in enumerate((0, 1, 3, 2)):
                xx = (x + dx) % X
                for way in range(2):
                    if step == 4 and way != i // 2:
                        continue
                    zz = (z + Z - step) % Z if way == 0 else (z + step) % Z
                    to = (z + 1) % Z if way == 0 else (z + Z - 1) % Z
                    q = piece0(zz, xx)
                    arrived(q, r_ring.at[way, (step - 1) * 4 + i])
                    if step < 3 or (step == 3 and way == i // 2):
                        send(q, q, s_ring.at[way, step * 4 + i], r_ring.at[way, step * 4 + i], dev(to, x, 0))
                    send(q, q, s_p.at[n], r_p.at[n], partner)
                    n += 1

    near = (0, 1, 7, 2, 6, 3, 5, 4)

    @pl.when(c == 1)
    def _():
        n = 0
        for i, dz in enumerate(near):
            zz = (z + dz) % Z
            for cc in range(2):
                if dz == 0 and cc == 1:
                    pltpu.make_async_copy(half1, mine1, s_loc.at[1]).wait()
                else:
                    arrived(g.at[1, zz, x, pl.ds(cc * 64, 64)], r_b.at[zz * 2 + cc])
            q = g.at[1, zz, x]
            for way, to in ((0, (x + 1) % X), (1, (x + X - 1) % X)):
                send(q, q, s_ring.at[way, i], r_ring.at[way, i], dev(z, to, 1))
            send(q, q, s_p.at[n], r_p.at[n], partner)
            n += 1
        for step in range(1, 3):
            for i, dz in enumerate(near):
                zz = (z + dz) % Z
                for way in range(2):
                    if step == 2 and way != i % 2:
                        continue
                    xx = (x + X - step) % X if way == 0 else (x + step) % X
                    to = (x + 1) % X if way == 0 else (x + X - 1) % X
                    q = g.at[1, zz, xx]
                    arrived(q, r_ring.at[way, (step - 1) * 8 + i])
                    if step == 1 and way == i % 2:
                        send(q, q, s_ring.at[way, step * 8 + i], r_ring.at[way, step * 8 + i], dev(z, to, 1))
                    send(q, q, s_p.at[n], r_p.at[n], partner)
                    n += 1

    for n in range(32):
        arrived(g.at[0, 0, 0], r_p.at[n])

    for k in range(8):
        pltpu.make_async_copy(jac_ref.at[:, pl.ds(k * 256, 256)], jv.at[k], s_jac.at[k]).wait()

    def image(i, _):
        rows = pl.ds(pl.multiple_of(i * 256, 256), 256)
        total = jnp.zeros((256, 256), F32)
        for k in range(8):
            t = lists_ref[k, obs]
            cols = jnp.concatenate([g[h, t // 2, pl.ds((t % 2) * 2, 2)].reshape(256, 128) for h in range(2)], axis=1)
            total += jnp.dot(jv[k, rows, :], cols, preferred_element_type=F32)
        turned = total.T
        for j in range(2):
            lane = lax.broadcasted_iota(jnp.int32, (1, 128), 1) + (y * 1024 + (i * 2 + j) * 128)
            weight = jnp.where(lane < count_ref[0], w_ref[pl.ds(i * 2 + j, 1), :], 0.0)
            img[:, pl.ds(pl.multiple_of(i * 256 + j * 128, 128), 128)] = (turned[:, j * 128:(j + 1) * 128] * weight).astype(BF16)
        return 0

    lax.fori_loop(0, 4, image, 0)

    low = lax.broadcasted_iota(jnp.int32, (1, 1, 128), 2) < 64

    def contribution(k, _):
        total = jnp.dot(img[...], jv[k], preferred_element_type=F32).reshape(4, 2, 32, 256)
        for b in range(2):
            up = total[:, 0, :, b * 128:(b + 1) * 128]
            down = total[:, 1, :, b * 128:(b + 1) * 128]
            first = jnp.where(low, up, pltpu.roll(down, 64, 2))
            second = jnp.where(low, pltpu.roll(up, 64, 2), down)
            cown[k, b] = jnp.where(c == 0, first, second)
            csend[k, b] = jnp.where(c == 0, second, first).astype(BF16)
        send(csend.at[k], crecv.at[k], s_c.at[k], r_c.at[k], partner)
        return 0

    lax.fori_loop(0, 8, contribution, 0)
    for k in range(8):
        arrived(crecv.at[k], r_c.at[k])

    def place(t, _):
        mine = cown[table[0, t]] * table[1, t].astype(F32)
        other = crecv[table[2, t]].astype(F32) * table[3, t].astype(F32)
        both = (mine + other).astype(BF16)
        for b in range(2):
            xx = 2 * (t % 2) + b
            for yy in range(4):
                d[jnp.where(c == 0, yy, xx), jnp.where(c == 0, xx, yy), t // 2] = both[b, yy]
        return 0

    lax.fori_loop(0, 16, place, 0)

    def along(axis, by):
        if axis == 0:
            return ((z * X + jnp.where(c == 0, x, (x + by) % X)) * 2 + c, jnp.where(c == 0, (y + by) % Y, y))
        return ((z * X + jnp.where(c == 0, (x + by) % X, x)) * 2 + c, jnp.where(c == 0, y, (y + by) % Y))

    def ring(axis, buf, here, lo, hi, ra, rb, rc):
        nxt, opp, prv = (here + 1) % 4, (here + 2) % 4, (here + 3) % 4
        right, left = along(axis, 1), along(axis, 3)
        o = axis * 6
        started = [
            send(buf.at[opp, lo], ra.at[0], s_q.at[o], r_q.at[o], right),
            send(buf.at[opp, hi], ra.at[1], s_q.at[o + 1], r_q.at[o + 1], left),
            send(buf.at[nxt, hi], rb.at[0], s_q.at[o + 2], r_q.at[o + 2], right),
            send(buf.at[prv, lo], rb.at[1], s_q.at[o + 3], r_q.at[o + 3], left),
        ]
        for i, (to, part, dst) in enumerate(((nxt, lo, right), (prv, hi, left))):
            arrived(ra.at[i], r_q.at[o + i])
            buf[to, part] = (buf[to, part].astype(F32) + ra[i].astype(F32)).astype(BF16)
            started.append(send(buf.at[to, part], rc.at[i], s_q.at[o + 4 + i], r_q.at[o + 4 + i], dst))
        arrived(rb.at[1], r_q.at[o + 3])
        arrived(rb.at[0], r_q.at[o + 2])
        arrived(rc.at[0], r_q.at[o + 4])
        arrived(rc.at[1], r_q.at[o + 5])
        return started

    first_here = jnp.where(c == 0, y, x)
    second_here = jnp.where(c == 0, x, y)
    lo, hi = pl.ds(0, 2), pl.ds(2, 2)
    started = ring(0, d, first_here, lo, hi, ra, rb, rc)
    e[lo] = (d[first_here, lo].astype(F32) + rc[0].astype(F32) + rb[1].astype(F32)).astype(BF16)
    e[hi] = (d[first_here, hi].astype(F32) + rb[0].astype(F32) + rc[1].astype(F32)).astype(BF16)

    lo, hi = pl.ds(0, 4), pl.ds(4, 4)
    ra2, rb2, rc2 = [r3.at[pl.ds(n * 2, 2)] for n in range(3)]
    started += ring(1, e, second_here, lo, hi, ra2, rb2, rc2)
    fin[lo] = e[second_here, lo].astype(F32) + rc2[0].astype(F32) + rb2[1].astype(F32)
    fin[hi] = e[second_here, hi].astype(F32) + rb2[0].astype(F32) + rc2[1].astype(F32)

    for dz in (4, 3, 5, 2, 6, 1, 7):
        started.append(send(fin.at[(z + dz) % Z], fin.at[8 + dz], s_z.at[dz], r_z.at[dz], dev((z + dz) % Z, x, c)))
    total = fin[z]
    for dz in (1, 7, 2, 6, 3, 5, 4):
        arrived(fin.at[8 + dz], r_z.at[dz])
        total = total + fin[8 + dz]
    turned = total.T
    out_ref[:, 0:32] = turned[0:64].astype(BF16)
    out_ref[:, 32:64] = turned[64:128].astype(BF16)

    for copy in started:
        copy.wait_send()
    for k in range(8):
        sent(csend.at[k], s_c.at[k])
    for dx in (1, 3, 2):
        sent(half0, s_a.at[dx])
    for dz in range(1, 8):
        sent(half1, s_b.at[dz])
    for n in range(32):
        sent(g.at[0, 0, 0], s_p.at[n])

    @pl.when(c == 0)
    def _():
        sent(half1, s_b.at[0])
        for way in range(2):
            for n in range(16):
                if n < 12 or (n - 12) // 2 == way:
                    sent(g.at[0, 0, 0], s_ring.at[way, n])

    @pl.when(c == 1)
    def _():
        sent(half0, s_a.at[0])
        for way in range(2):
            for n in range(16):
                if n < 8 or n % 2 == way:
                    sent(g.at[0, 0, 0], s_ring.at[way, n])


def local(jacobian, obs_weight, row_counts, tile_lists, tile_slot, probe_block):
    smem, vmem, hbm = (pl.BlockSpec(memory_space=m) for m in (pltpu.SMEM, pltpu.VMEM, pl.ANY))
    dma = lambda *shape: pltpu.SemaphoreType.DMA(shape)
    return pl.pallas_call(
        kernel,
        out_shape=jax.ShapeDtypeStruct((64, 64), BF16),
        in_specs=[smem, smem, smem, vmem, hbm, hbm],
        out_specs=vmem,
        scratch_shapes=[
            pltpu.SMEM((4, 16), jnp.int32),
            pltpu.VMEM((64, 256), BF16),
            pltpu.VMEM((8, 1024, 256), BF16),
            pltpu.VMEM((2, Z, X, 128, 128), BF16),
            pltpu.VMEM((256, 1024), BF16),
            pltpu.VMEM((8, 2, 4, 32, 128), F32),
            pltpu.VMEM((8, 2, 4, 32, 128), BF16),
            pltpu.VMEM((8, 2, 4, 32, 128), BF16),
            pltpu.VMEM((4, 4, 8, 32, 128), BF16),
            pltpu.VMEM((2, 2, 8, 32, 128), BF16),
            pltpu.VMEM((2, 2, 8, 32, 128), BF16),
            pltpu.VMEM((2, 2, 8, 32, 128), BF16),
            pltpu.VMEM((4, 8, 32, 128), BF16),
            pltpu.VMEM((6, 4, 32, 128), BF16),
            pltpu.VMEM((16, 32, 128), F32),
            dma(3), dma(8), dma(4), dma(8), dma(8), dma(16), dma(2, 16), dma(2, 16), dma(32), dma(32), dma(8), dma(8),
            dma(12), dma(12), dma(8), dma(8),
        ],
        compiler_params=pltpu.CompilerParams(collective_id=0, has_side_effects=True, vmem_limit_bytes=60 * 1024 * 1024),
    )(tile_lists.T, tile_slot, row_counts, obs_weight.reshape(8, 128), jacobian, probe_block)


def solution(mesh):
    placed = (P(("obs", "sub"), None), P(("obs", "sub")), P("obs"), P(), P(), P("obs", None))
    return jax.shard_map(local, mesh=mesh, in_specs=placed, out_specs=P("obs", "sub"), check_vma=False)
```

time: 301 us -> 60.1 us (0.20)
  waiting for transfers between devices: 253 us -> 0 us
  Pallas kernels: 0 us -> 57.9 us
  matrix products: 16.3 us -> 0 us
  between operations: 13.8 us -> 0.66 us
  local copies, waits for them, and re-layouts: 12.9 us -> 1.32 us
  other arithmetic: 5.19 us -> 0 us
    reduce_scatter x2 -> x0, waiting for transfers between devices: 170 us -> none  [the longest x1 143 us: local(): lax.psum_scatter(taken * found[:, None].astype(jnp.float32), 'obs', scatt...]
    all_gather x1 -> x0, waiting for transfers between devices: 81.4 us -> none  [local(): piece = lax.all_gather(probe_block, 'obs', axis=0, tiled=True)]
    pallas_call x0 -> x1, Pallas kernels: none -> 57.9 us  [local(): pl.pallas_call(kernel, out_shape=jax.ShapeDtypeStruct((64, 64), BF16), in...]
    dot_general x2 -> x0, matrix products: 16.3 us -> none  [the longest x1 11.4 us: local(): jnp.dot(jacobian, probe_cols, preferred_element_type=jnp.float32)]
    gather x1 -> x0, local copies, waits for them, and re-layouts: 10.8 us -> none  [local(): taken = jnp.take(block_sum, source_rows, axis=0)]
    mul x4 -> x0, other arithmetic: 3.36 us -> none  [the longest x1 2.66 us: local(): taken * found[:, None].astype(jnp.float32)]
  transfers between devices with their start and end apart: 3 -> 0, of which waited for: 3 -> 0; matrix products, arithmetic and copies ran while one was open for 0% -> 0% of each run, Pallas kernels for 0% -> 0%
where the time goes in v1:
time: 60.1 us; the launch traced here: 59.9 us
  Pallas kernels  57.9 us (96%)
  local copies, waits for them, and re-layouts  1.32 us (2%)
  between operations  0.66 us (1%)
    pallas_call x1, Pallas kernels, local(): pl.pallas_call(kernel, out_shape=jax.ShapeDtypeStruct((64, 64), BF16), in...  57.9 us
    unnamed x1, local copies, waits for them, and re-layouts  1.32 us

profile of v1, /device:TPU:8, one launch (start us, length us, event | category | flops | bytes accessed | tf_op | source)
XLA Modules:
  0.0 59.9 jit_solution(11420221643691863094)
XLA Ops:
  0.7 57.9 %shard_map.64 = bf16[64,64]{1,0:T(8,128)(2,1)} custom-call(s32[8,64]{1,0:T(8,128)} %bitcast.2, s32[16]{0:T(128)} %slot_ref.1, s32[1]{0:T(128)S(6)} %copy.8.count_ref, f32[8,128]{1,0:T(8,128)} %bitcast.3, bf16[1024,2048]{1,0:T(8,128)(2,1)} %jac_ref.1, bf16[64,256]{1,0:T(8,128)(2,1)} %probe_ref.1), custom_call_target="tpu_custom_call" | custom-call | tf_op jit(solution)/shard_map/pallas_call | solution.py:281
  58.5 1.3 %copy.9 = bf16[64,64]{1,0:T(8,128)(2,1)} copy(bf16[64,64]{1,0:T(8,128)(2,1)} %shard_map.64) | data formatting | bytes 16384

commit v2 on v0

v2 whole, which is shorter than its diff:
```python
import jax
import jax.numpy as jnp
from jax import lax
from jax.experimental import pallas as pl
from jax.experimental.pallas import tpu as pltpu
from jax.sharding import PartitionSpec as P

MESH = pl.DeviceIdType.MESH
X, Y, Z = 4, 4, 8
F32, BF16 = jnp.float32, jnp.bfloat16
NEAR = (1, 7, 2, 6, 3, 5, 4)
FAR = (4, 3, 5, 2, 6, 1, 7)


def kernel(lists_hbm, slot_hbm, count_hbm, w_hbm, jac_ref, probe_ref, out_ref,
           lists_ref, slot_ref, count_ref, table, w_ref, jv, g, img, cown, csend, crecv, d, r1, e, r2, fin, r3,
           s_in, s_jac, s_gz, r_gz, s_gx, r_gx, s_gp, r_gp, s_gb, r_gb, s_gq, r_gq, s_c, r_c, s_1, r_1, s_2, r_2, s_3, r_3):
    obs, y = lax.axis_index("obs"), lax.axis_index("sub")
    c = obs % 2
    x = (obs // 2) % X
    z = obs // (2 * X)

    def dev(zz, xx, cc):
        return ((zz * X + xx) * 2 + cc, y)

    partner = dev(z, x, 1 - c)
    role = 1 - c
    log = [[]]

    def remote(src, dst, s, r, to):
        return pltpu.make_async_remote_copy(src_ref=src, dst_ref=dst, send_sem=s, recv_sem=r, device_id=to, device_id_type=MESH)

    def send(src, dst, s, r, to):
        copy = remote(src, dst, s, r, to)
        copy.start()
        log[-1].append(copy)

    def arrived(dst, r):
        remote(dst, dst, s_in.at[0], r, partner).wait_recv()

    mine = g.at[z, x, c]
    inputs = [pltpu.make_async_copy(src, dst, s_in.at[i]) for i, (src, dst) in enumerate(
        ((probe_ref, mine), (lists_hbm, lists_ref), (slot_hbm, slot_ref), (count_hbm, count_ref), (w_hbm, w_ref)))]
    for copy in inputs:
        copy.start()
    jacs = [pltpu.make_async_copy(jac_ref.at[:, pl.ds(k * 256, 256)], jv.at[k], s_jac.at[k]) for k in range(8)]
    for copy in jacs:
        copy.start()

    def along(axis, by):
        dx = jnp.where(role == axis, 0, by)
        dy = jnp.where(role == axis, by, 0)
        return ((z * X + (x + dx) % X) * 2 + c, (y + dy) % Y)

    first = jnp.where(role == 0, y, x)
    second = jnp.where(role == 0, x, y)

    barrier = pltpu.get_barrier_semaphore()
    others = [dev((z + dz) % Z, x, c) for dz in range(1, Z)] + [partner]
    others += [along(axis, by) for axis in range(2) for by in range(1, 4)]
    for o in others:
        pl.semaphore_signal(barrier, inc=1, device_id=o, device_id_type=MESH)
    inputs[0].wait()
    pl.semaphore_wait(barrier, len(others))

    xo = (x + 2) % X

    def source(n):
        return (z + Z - ((0,) + NEAR)[n]) % Z

    def top(zz, xx):
        return g.at[zz, xx, c, pl.ds(0, 32)]

    def bottom(zz, xx):
        return g.at[zz, xx, c, pl.ds(32, 32)]

    def along_x(dx, zz, xx, n):
        return top(zz, xx) if dx == 2 and n else g.at[zz, xx, c]

    for dz in NEAR:
        send(mine, mine, s_gz.at[dz], r_gz.at[dz], dev((z + dz) % Z, x, c))

    def spread(n):
        zz = source(n)
        for dx in (1, 3, 2):
            q = along_x(dx, zz, x, n)
            send(q, q, s_gx.at[dx, n], r_gx.at[dx, n], dev(z, (x + dx) % X, c))
        q = g.at[zz, x, c]
        send(q, q, s_gp.at[0, n], r_gp.at[0, n], partner)

    spread(0)

    for n in range(1, 8):
        if n == 4:
            q = g.at[z, xo, c]
            arrived(q, r_gx.at[2, 0])
            for dz in NEAR:
                send(bottom(z, xo), bottom(z, xo), s_gb.at[dz], r_gb.at[dz], dev((z + dz) % Z, x, c))
            send(q, q, s_gp.at[2, 0], r_gp.at[2, 0], partner)
        arrived(g.at[source(n), x, c], r_gz.at[NEAR[n - 1]])
        spread(n)
    for n in range(8):
        zz = source(n)
        for dx in (1, 3, 2) if n else (1, 3):
            q = along_x(dx, zz, (x + X - dx) % X, n)
            arrived(q, r_gx.at[dx, n])
            send(q, q, s_gp.at[dx, n], r_gp.at[dx, n], partner)
        if n:
            q = bottom(zz, xo)
            arrived(q, r_gb.at[NEAR[n - 1]])
            send(q, q, s_gq.at[n], r_gq.at[n], partner)
    for copy in inputs[1:]:
        copy.wait()

    def fill(t, _):
        for which, owner in enumerate((obs, obs + 1 - 2 * c)):
            at, found = jnp.int32(0), jnp.int32(0)
            for k in range(8):
                hit = slot_ref[lists_ref[k, owner]] == t
                at = jnp.where(hit, k, at)
                found = jnp.where(hit, 1, found)
            table[2 * which, t] = at
            table[2 * which + 1, t] = found
        return 0

    lax.fori_loop(0, 16, fill, 0)

    for copy in jacs:
        copy.wait()
    for n in range(8):
        for dx in (0, 1, 3, 2):
            arrived(along_x(dx, z, x, n), r_gp.at[dx, n])
        if n:
            arrived(bottom(z, x), r_gq.at[n])

    def image(i, _):
        rows = pl.ds(pl.multiple_of(i * 256, 256), 256)
        total = jnp.zeros((256, 256), F32)
        for k in range(8):
            t = lists_ref[k, obs]
            cols = g[t // 2, pl.ds((t % 2) * 2, 2)].reshape(256, 256)
            total += jnp.dot(jv[k, rows, :], cols, preferred_element_type=F32)
        turned = total.T
        for j in range(2):
            lane = lax.broadcasted_iota(jnp.int32, (1, 128), 1) + (y * 1024 + (i * 2 + j) * 128)
            weight = jnp.where(lane < count_ref[0], w_ref[pl.ds(i * 2 + j, 1), :], 0.0)
            img[:, pl.ds(pl.multiple_of(i * 256 + j * 128, 128), 128)] = (turned[:, j * 128:(j + 1) * 128] * weight).astype(BF16)
        return 0

    lax.fori_loop(0, 4, image, 0, unroll=2)

    low = lax.broadcasted_iota(jnp.int32, (1, 1, 128), 2) < 64

    def contribution(k, _):
        total = jnp.dot(img[...], jv[k], preferred_element_type=F32).reshape(4, 2, 32, 256)
        for b in range(2):
            up = total[:, 0, :, b * 128:(b + 1) * 128]
            down = total[:, 1, :, b * 128:(b + 1) * 128]
            one = jnp.where(low, up, pltpu.roll(down, 64, 2))
            two = jnp.where(low, pltpu.roll(up, 64, 2), down)
            cown[k, b] = jnp.where(c == 0, one, two)
            csend[k, b] = jnp.where(c == 0, two, one).astype(BF16)
        remote(csend.at[k], crecv.at[k], s_c.at[k], r_c.at[k], partner).start()
        return 0

    lax.fori_loop(0, 8, contribution, 0)
    for k in range(8):
        arrived(crecv.at[k], r_c.at[k])

    def chip_sum(t, part):
        own = cown[(table[0, t],) + part] * table[1, t].astype(F32)
        other = crecv[(table[2, t],) + part].astype(F32) * table[3, t].astype(F32)
        return (own + other).astype(BF16)

    gathered = log[-1]
    log.append([])

    for by2 in (2, 1, 3, 0):
        s = (second + by2) % 4

        @pl.when(role == 0)
        def _():
            def place(zz, _):
                d[:, s, zz] = chip_sum(2 * zz + s // 2, (s % 2,))
                return 0

            lax.fori_loop(0, 8, place, 0)

        @pl.when(role == 1)
        def _():
            def place(t, _):
                both = chip_sum(t, (slice(None), s))
                for b in range(2):
                    d[2 * (t % 2) + b, s, t // 2] = both[b]
                return 0

            lax.fori_loop(0, 16, place, 0)

        for by in (2, 1, 3):
            send(d.at[(first + by) % 4, s], r1.at[by, by2], s_1.at[by, by2], r_1.at[by, by2], along(0, by))

    for copy in gathered:
        copy.wait_send()
    for k in range(8):
        remote(csend.at[k], crecv.at[k], s_c.at[k], r_c.at[k], partner).wait_send()

    for by2 in (2, 1, 3, 0):
        s = (second + by2) % 4
        for by in (1, 3, 2):
            arrived(r1.at[by, by2], r_1.at[by, by2])
        total = d[first, s].astype(F32) + r1[1, by2].astype(F32) + r1[3, by2].astype(F32) + r1[2, by2].astype(F32)
        if by2:
            e[by2] = total.astype(BF16)
        else:
            fin[...] = total
        if by2:
            send(e.at[by2], r2.at[by2], s_2.at[by2], r_2.at[by2], along(1, by2))
    for by2 in (1, 3, 2):
        arrived(r2.at[by2], r_2.at[by2])

    for dz in FAR:
        zz = (z + dz) % Z
        fin[zz] = fin[zz] + r2[1, zz].astype(F32) + r2[3, zz].astype(F32) + r2[2, zz].astype(F32)
        send(fin.at[zz], r3.at[dz], s_3.at[dz], r_3.at[dz], dev(zz, x, c))
    total = fin[z] + r2[1, z].astype(F32) + r2[3, z].astype(F32) + r2[2, z].astype(F32)
    for dz in NEAR:
        arrived(r3.at[dz], r_3.at[dz])
        total = total + r3[dz]
    turned = total.T
    out_ref[:, 0:32] = turned[0:64].astype(BF16)
    out_ref[:, 32:64] = turned[64:128].astype(BF16)

    for copy in log[-1]:
        copy.wait_send()


def local(jacobian, obs_weight, row_counts, tile_lists, tile_slot, probe_block):
    dma = lambda *shape: pltpu.SemaphoreType.DMA(shape)
    return pl.pallas_call(
        kernel,
        out_shape=jax.ShapeDtypeStruct((64, 64), BF16),
        in_specs=[pl.BlockSpec(memory_space=pl.ANY)] * 6,
        out_specs=pl.BlockSpec(memory_space=pltpu.VMEM),
        scratch_shapes=[
            pltpu.SMEM((8, 64), jnp.int32),
            pltpu.SMEM((16,), jnp.int32),
            pltpu.SMEM((1,), jnp.int32),
            pltpu.SMEM((4, 16), jnp.int32),
            pltpu.VMEM((8, 128), F32),
            pltpu.VMEM((8, 1024, 256), BF16),
            pltpu.VMEM((Z, X, 2, 64, 256), BF16),
            pltpu.VMEM((256, 1024), BF16),
            pltpu.VMEM((8, 2, 4, 32, 128), F32),
            pltpu.VMEM((8, 2, 4, 32, 128), BF16),
            pltpu.VMEM((8, 2, 4, 32, 128), BF16),
            pltpu.VMEM((4, 4, 8, 32, 128), BF16),
            pltpu.VMEM((4, 4, 8, 32, 128), BF16),
            pltpu.VMEM((4, 8, 32, 128), BF16),
            pltpu.VMEM((4, 8, 32, 128), BF16),
            pltpu.VMEM((8, 32, 128), F32),
            pltpu.VMEM((8, 32, 128), F32),
            dma(5), dma(8), dma(8), dma(8), dma(4, 8), dma(4, 8), dma(4, 8), dma(4, 8),
            dma(8), dma(8), dma(8), dma(8), dma(8), dma(8),
            dma(4, 4), dma(4, 4), dma(4), dma(4), dma(8), dma(8),
        ],
        compiler_params=pltpu.CompilerParams(collective_id=0, has_side_effects=True, vmem_limit_bytes=60 * 1024 * 1024),
    )(tile_lists.T, tile_slot, row_counts, obs_weight.reshape(8, 128), jacobian, probe_block)


def solution(mesh):
    placed = (P(("obs", "sub"), None), P(("obs", "sub")), P("obs"), P(), P(), P("obs", None))
    return jax.shard_map(local, mesh=mesh, in_specs=placed, out_specs=P("obs", "sub"), check_vma=False)
```

time: 301 us -> 51.4 us (0.17)
  waiting for transfers between devices: 253 us -> 0 us
  Pallas kernels: 0 us -> 49.1 us
  matrix products: 16.3 us -> 0 us
  between operations: 13.8 us -> 0.66 us
  local copies, waits for them, and re-layouts: 12.9 us -> 1.32 us
  other arithmetic: 5.19 us -> 0 us
    reduce_scatter x2 -> x0, waiting for transfers between devices: 170 us -> none  [the longest x1 143 us: local(): lax.psum_scatter(taken * found[:, None].astype(jnp.float32), 'obs', scatt...]
    all_gather x1 -> x0, waiting for transfers between devices: 81.4 us -> none  [local(): piece = lax.all_gather(probe_block, 'obs', axis=0, tiled=True)]
    pallas_call x0 -> x1, Pallas kernels: none -> 49.1 us  [local(): pl.pallas_call(kernel, out_shape=jax.ShapeDtypeStruct((64, 64), BF16), in...]
    dot_general x2 -> x0, matrix products: 16.3 us -> none  [the longest x1 11.4 us: local(): jnp.dot(jacobian, probe_cols, preferred_element_type=jnp.float32)]
    gather x1 -> x0, local copies, waits for them, and re-layouts: 10.8 us -> none  [local(): taken = jnp.take(block_sum, source_rows, axis=0)]
    mul x4 -> x0, other arithmetic: 3.36 us -> none  [the longest x1 2.66 us: local(): taken * found[:, None].astype(jnp.float32)]
  transfers between devices with their start and end apart: 3 -> 0, of which waited for: 3 -> 0; matrix products, arithmetic and copies ran while one was open for 0% -> 0% of each run, Pallas kernels for 0% -> 0%
where the time goes in v2:
time: 51.4 us; the launch traced here: 51.1 us
  Pallas kernels  49.1 us (96%)
  local copies, waits for them, and re-layouts  1.32 us (3%)
  between operations  0.66 us (1%)
    pallas_call x1, Pallas kernels, local(): pl.pallas_call(kernel, out_shape=jax.ShapeDtypeStruct((64, 64), BF16), in...  49.1 us
    unnamed x1, local copies, waits for them, and re-layouts  1.32 us

profile of v2, /device:TPU:8, one launch (start us, length us, event | category | flops | bytes accessed | tf_op | source)
XLA Modules:
  0.0 51.1 jit_solution(13964941116912129395)
XLA Ops:
  0.7 49.1 %shard_map.64 = bf16[64,64]{1,0:T(8,128)(2,1)} custom-call(s32[8,64]{1,0:T(8,128)} %bitcast.2, s32[16]{0:T(128)} %slot_hbm.1, s32[1]{0:T(128)S(6)} %copy.8.count_hbm, f32[8,128]{1,0:T(8,128)} %bitcast.3, bf16[1024,2048]{1,0:T(8,128)(2,1)} %jac_ref.1, bf16[64,256]{1,0:T(8,128)(2,1)} %probe_ref.1), custom_call_target="tpu_custom_call" | custom-call | tf_op jit(solution)/shard_map/pallas_call | solution.py:239
  49.8 1.3 %copy.9 = bf16[64,64]{1,0:T(8,128)(2,1)} copy(bf16[64,64]{1,0:T(8,128)(2,1)} %shard_map.64) | data formatting | bytes 16384

commit v3 on v2

--- a/solution.py
+++ b/solution.py
@@ -10,11 +10,12 @@
 F32, BF16 = jnp.float32, jnp.bfloat16
 NEAR = (1, 7, 2, 6, 3, 5, 4)
 FAR = (4, 3, 5, 2, 6, 1, 7)
+TURNED = (1, 2, 3, 4)
 
 
 def kernel(lists_hbm, slot_hbm, count_hbm, w_hbm, jac_ref, probe_ref, out_ref,
-           lists_ref, slot_ref, count_ref, table, w_ref, jv, g, img, cown, csend, crecv, d, r1, e, r2, fin, r3,
-           s_in, s_jac, s_gz, r_gz, s_gx, r_gx, s_gp, r_gp, s_gb, r_gb, s_gq, r_gq, s_c, r_c, s_1, r_1, s_2, r_2, s_3, r_3):
+           lists_ref, slot_ref, count_ref, table, w_ref, jv, g, img, cown, csend, crecv, d, r1, e, r2, fin, fout, r3, ro, so, rf,
+           s_in, s_jac, s_gz, r_gz, s_gx, r_gx, s_gp, r_gp, s_go, r_go, s_c, r_c, s_1, r_1, s_2, r_2, s_3, r_3, s_o, r_o, s_f, r_f):
     obs, y = lax.axis_index("obs"), lax.axis_index("sub")
     c = obs % 2
     x = (obs // 2) % X
@@ -48,8 +49,11 @@
         copy.start()
 
     def along(axis, by):
-        dx = jnp.where(role == axis, 0, by)
-        dy = jnp.where(role == axis, by, 0)
+        return at(by, 0) if axis == 0 else at(0, by)
+
+    def at(by, by2):
+        dx = jnp.where(role == 0, by2, by)
+        dy = jnp.where(role == 0, by, by2)
         return ((z * X + (x + dx) % X) * 2 + c, (y + dy) % Y)
 
     first = jnp.where(role == 0, y, x)
@@ -57,7 +61,7 @@
 
     barrier = pltpu.get_barrier_semaphore()
     others = [dev((z + dz) % Z, x, c) for dz in range(1, Z)] + [partner]
-    others += [along(axis, by) for axis in range(2) for by in range(1, 4)]
+    others += [along(axis, by) for axis in range(2) for by in range(1, 4)] + [at(2, by2) for by2 in range(1, 4)]
     for o in others:
         pl.semaphore_signal(barrier, inc=1, device_id=o, device_id_type=MESH)
     inputs[0].wait()
@@ -68,47 +72,36 @@
     def source(n):
         return (z + Z - ((0,) + NEAR)[n]) % Z
 
-    def top(zz, xx):
-        return g.at[zz, xx, c, pl.ds(0, 32)]
-
-    def bottom(zz, xx):
-        return g.at[zz, xx, c, pl.ds(32, 32)]
-
-    def along_x(dx, zz, xx, n):
-        return top(zz, xx) if dx == 2 and n else g.at[zz, xx, c]
+    def hand_over(dx, n, r):
+        q = g.at[source(n), (x + X - dx) % X, c]
+        arrived(q, r)
+        send(q, q, s_gp.at[dx, n], r_gp.at[dx, n], partner)
+
+    def spread(n):
+        q = g.at[source(n), x, c]
+        for dx in (1, 3) if n in TURNED else (1, 3, 2):
+            send(q, q, s_gx.at[dx, n], r_gx.at[dx, n], dev(z, (x + dx) % X, c))
+        send(q, q, s_gp.at[0, n], r_gp.at[0, n], partner)
 
     for dz in NEAR:
         send(mine, mine, s_gz.at[dz], r_gz.at[dz], dev((z + dz) % Z, x, c))
-
-    def spread(n):
-        zz = source(n)
-        for dx in (1, 3, 2):
-            q = along_x(dx, zz, x, n)
-            send(q, q, s_gx.at[dx, n], r_gx.at[dx, n], dev(z, (x + dx) % X, c))
-        q = g.at[zz, x, c]
-        send(q, q, s_gp.at[0, n], r_gp.at[0, n], partner)
-
     spread(0)
-
     for n in range(1, 8):
         if n == 4:
             q = g.at[z, xo, c]
             arrived(q, r_gx.at[2, 0])
-            for dz in NEAR:
-                send(bottom(z, xo), bottom(z, xo), s_gb.at[dz], r_gb.at[dz], dev((z + dz) % Z, x, c))
+            for dz in [NEAR[i - 1] for i in TURNED]:
+                send(q, q, s_go.at[dz], r_go.at[dz], dev((z + dz) % Z, x, c))
             send(q, q, s_gp.at[2, 0], r_gp.at[2, 0], partner)
+        if n == 3:
+            for dx in (1, 3):
+                hand_over(dx, 0, r_gx.at[dx, 0])
         arrived(g.at[source(n), x, c], r_gz.at[NEAR[n - 1]])
         spread(n)
-    for n in range(8):
-        zz = source(n)
-        for dx in (1, 3, 2) if n else (1, 3):
-            q = along_x(dx, zz, (x + X - dx) % X, n)
-            arrived(q, r_gx.at[dx, n])
-            send(q, q, s_gp.at[dx, n], r_gp.at[dx, n], partner)
-        if n:
-            q = bottom(zz, xo)
-            arrived(q, r_gb.at[NEAR[n - 1]])
-            send(q, q, s_gq.at[n], r_gq.at[n], partner)
+    for n in range(1, 8):
+        for dx in (1, 3):
+            hand_over(dx, n, r_gx.at[dx, n])
+        hand_over(2, n, r_go.at[NEAR[n - 1]] if n in TURNED else r_gx.at[2, n])
     for copy in inputs[1:]:
         copy.wait()
 
@@ -129,9 +122,7 @@
         copy.wait()
     for n in range(8):
         for dx in (0, 1, 3, 2):
-            arrived(along_x(dx, z, x, n), r_gp.at[dx, n])
-        if n:
-            arrived(bottom(z, x), r_gq.at[n])
+            arrived(mine, r_gp.at[dx, n])
 
     def image(i, _):
         rows = pl.ds(pl.multiple_of(i * 256, 256), 256)
@@ -196,8 +187,12 @@
 
             lax.fori_loop(0, 16, place, 0)
 
-        for by in (2, 1, 3):
+        for by in (1, 3):
             send(d.at[(first + by) % 4, s], r1.at[by, by2], s_1.at[by, by2], r_1.at[by, by2], along(0, by))
+
+    opposite = (first + 2) % 4
+    for dz in NEAR:
+        send(d.at[opposite, :, (z + dz) % Z], ro.at[dz], s_o.at[dz], r_o.at[dz], dev((z + dz) % Z, x, c))
 
     for copy in gathered:
         copy.wait_send()
@@ -206,9 +201,9 @@
 
     for by2 in (2, 1, 3, 0):
         s = (second + by2) % 4
-        for by in (1, 3, 2):
+        for by in (1, 3):
             arrived(r1.at[by, by2], r_1.at[by, by2])
-        total = d[first, s].astype(F32) + r1[1, by2].astype(F32) + r1[3, by2].astype(F32) + r1[2, by2].astype(F32)
+        total = d[first, s].astype(F32) + r1[1, by2].astype(F32) + r1[3, by2].astype(F32)
         if by2:
             e[by2] = total.astype(BF16)
         else:
@@ -220,12 +215,23 @@
 
     for dz in FAR:
         zz = (z + dz) % Z
-        fin[zz] = fin[zz] + r2[1, zz].astype(F32) + r2[3, zz].astype(F32) + r2[2, zz].astype(F32)
-        send(fin.at[zz], r3.at[dz], s_3.at[dz], r_3.at[dz], dev(zz, x, c))
+        total = fin[zz] + r2[1, zz].astype(F32) + r2[3, zz].astype(F32) + r2[2, zz].astype(F32)
+        fout[dz] = total.astype(BF16)
+        send(fout.at[dz], r3.at[dz], s_3.at[dz], r_3.at[dz], dev(zz, x, c))
     total = fin[z] + r2[1, z].astype(F32) + r2[3, z].astype(F32) + r2[2, z].astype(F32)
+    across = d[opposite, :, z].astype(F32)
+    for dz in NEAR:
+        arrived(ro.at[dz], r_o.at[dz])
+        across = across + ro[dz].astype(F32)
+    so[...] = across
+    for by2 in (2, 1, 3, 0):
+        send(so.at[(second + by2) % 4], rf.at[by2], s_f.at[by2], r_f.at[by2], at(2, by2))
     for dz in NEAR:
         arrived(r3.at[dz], r_3.at[dz])
-        total = total + r3[dz]
+        total = total + r3[dz].astype(F32)
+    for by2 in (0, 1, 3, 2):
+        arrived(rf.at[by2], r_f.at[by2])
+        total = total + rf[by2]
     turned = total.T
     out_ref[:, 0:32] = turned[0:64].astype(BF16)
     out_ref[:, 32:64] = turned[64:128].astype(BF16)
@@ -258,10 +264,14 @@
             pltpu.VMEM((4, 8, 32, 128), BF16),
             pltpu.VMEM((4, 8, 32, 128), BF16),
             pltpu.VMEM((8, 32, 128), F32),
-            pltpu.VMEM((8, 32, 128), F32),
+            pltpu.VMEM((8, 32, 128), BF16),
+            pltpu.VMEM((8, 32, 128), BF16),
+            pltpu.VMEM((8, 4, 32, 128), BF16),
+            pltpu.VMEM((4, 32, 128), F32),
+            pltpu.VMEM((4, 32, 128), F32),
             dma(5), dma(8), dma(8), dma(8), dma(4, 8), dma(4, 8), dma(4, 8), dma(4, 8),
-            dma(8), dma(8), dma(8), dma(8), dma(8), dma(8),
-            dma(4, 4), dma(4, 4), dma(4), dma(4), dma(8), dma(8),
+            dma(8), dma(8), dma(8), dma(8),
+            dma(4, 4), dma(4, 4), dma(4), dma(4), dma(8), dma(8), dma(8), dma(8), dma(4), dma(4),
         ],
         compiler_params=pltpu.CompilerParams(collective_id=0, has_side_effects=True, vmem_limit_bytes=60 * 1024 * 1024),
     )(tile_lists.T, tile_slot, row_counts, obs_weight.reshape(8, 128), jacobian, probe_block)

time: 51.4 us -> 50.1 us (0.975)
  Pallas kernels: 49.1 us -> 47.9 us
    pallas_call x1, Pallas kernels: 49.1 us -> 47.9 us  [local(): pl.pallas_call(kernel, out_shape=jax.ShapeDtypeStruct((64, 64), BF16), in...]
where the time goes in v3:
time: 50.1 us; the launch traced here: 49.9 us
  Pallas kernels  47.9 us (96%)
  local copies, waits for them, and re-layouts  1.32 us (3%)
  between operations  0.66 us (1%)
    pallas_call x1, Pallas kernels, local(): pl.pallas_call(kernel, out_shape=jax.ShapeDtypeStruct((64, 64), BF16), in...  47.9 us
    unnamed x1, local copies, waits for them, and re-layouts  1.32 us

profile of v3, /device:TPU:8, one launch (start us, length us, event | category | flops | bytes accessed | tf_op | source)
XLA Modules:
  0.0 49.9 jit_solution(3511555986114918868)
XLA Ops:
  0.7 47.9 %shard_map.64 = bf16[64,64]{1,0:T(8,128)(2,1)} custom-call(s32[8,64]{1,0:T(8,128)} %bitcast.2, s32[16]{0:T(128)} %slot_hbm.1, s32[1]{0:T(128)S(6)} %copy.8.count_hbm, f32[8,128]{1,0:T(8,128)} %bitcast.3, bf16[1024,2048]{1,0:T(8,128)(2,1)} %jac_ref.1, bf16[64,256]{1,0:T(8,128)(2,1)} %probe_ref.1), custom_call_target="tpu_custom_call" | custom-call | tf_op jit(solution)/shard_map/pallas_call | solution.py:245
  48.6 1.3 %copy.9 = bf16[64,64]{1,0:T(8,128)(2,1)} copy(bf16[64,64]{1,0:T(8,128)(2,1)} %shard_map.64) | data formatting | bytes 16384

commit v4 on v3

--- a/solution.py
+++ b/solution.py
@@ -10,7 +10,7 @@
 F32, BF16 = jnp.float32, jnp.bfloat16
 NEAR = (1, 7, 2, 6, 3, 5, 4)
 FAR = (4, 3, 5, 2, 6, 1, 7)
-TURNED = (1, 2, 3, 4)
+TURNED = (1, 2)
 
 
 def kernel(lists_hbm, slot_hbm, count_hbm, w_hbm, jac_ref, probe_ref, out_ref,
@@ -223,7 +223,7 @@
     for dz in NEAR:
         arrived(ro.at[dz], r_o.at[dz])
         across = across + ro[dz].astype(F32)
-    so[...] = across
+    so[...] = across.astype(BF16)
     for by2 in (2, 1, 3, 0):
         send(so.at[(second + by2) % 4], rf.at[by2], s_f.at[by2], r_f.at[by2], at(2, by2))
     for dz in NEAR:
@@ -231,7 +231,7 @@
         total = total + r3[dz].astype(F32)
     for by2 in (0, 1, 3, 2):
         arrived(rf.at[by2], r_f.at[by2])
-        total = total + rf[by2]
+        total = total + rf[by2].astype(F32)
     turned = total.T
     out_ref[:, 0:32] = turned[0:64].astype(BF16)
     out_ref[:, 32:64] = turned[64:128].astype(BF16)
@@ -267,8 +267,8 @@
             pltpu.VMEM((8, 32, 128), BF16),
             pltpu.VMEM((8, 32, 128), BF16),
             pltpu.VMEM((8, 4, 32, 128), BF16),
-            pltpu.VMEM((4, 32, 128), F32),
-            pltpu.VMEM((4, 32, 128), F32),
+            pltpu.VMEM((4, 32, 128), BF16),
+            pltpu.VMEM((4, 32, 128), BF16),
             dma(5), dma(8), dma(8), dma(8), dma(4, 8), dma(4, 8), dma(4, 8), dma(4, 8),
             dma(8), dma(8), dma(8), dma(8),
             dma(4, 4), dma(4, 4), dma(4), dma(4), dma(8), dma(8), dma(8), dma(8), dma(4), dma(4),

time: 50.1 us -> 49.4 us (0.986)
  Pallas kernels: 47.9 us -> 46.9 us
    pallas_call x1, Pallas kernels: 47.9 us -> 46.9 us  [local(): pl.pallas_call(kernel, out_shape=jax.ShapeDtypeStruct((64, 64), BF16), in...]
where the time goes in v4:
time: 49.4 us; the launch traced here: 48.9 us
  Pallas kernels  46.9 us (95%)
  local copies, waits for them, and re-layouts  1.32 us (3%)
  between operations  0.66 us (1%)
    pallas_call x1, Pallas kernels, local(): pl.pallas_call(kernel, out_shape=jax.ShapeDtypeStruct((64, 64), BF16), in...  46.9 us
    unnamed x1, local copies, waits for them, and re-layouts  1.32 us

profile of v4, /device:TPU:8, one launch (start us, length us, event | category | flops | bytes accessed | tf_op | source)
XLA Modules:
  0.0 48.9 jit_solution(15984693812064243564)
XLA Ops:
  0.7 46.9 %shard_map.64 = bf16[64,64]{1,0:T(8,128)(2,1)} custom-call(s32[8,64]{1,0:T(8,128)} %bitcast.2, s32[16]{0:T(128)} %slot_hbm.1, s32[1]{0:T(128)S(6)} %copy.8.count_hbm, f32[8,128]{1,0:T(8,128)} %bitcast.3, bf16[1024,2048]{1,0:T(8,128)(2,1)} %jac_ref.1, bf16[64,256]{1,0:T(8,128)(2,1)} %probe_ref.1), custom_call_target="tpu_custom_call" | custom-call | tf_op jit(solution)/shard_map/pallas_call | solution.py:245
  47.5 1.3 %copy.9 = bf16[64,64]{1,0:T(8,128)(2,1)} copy(bf16[64,64]{1,0:T(8,128)(2,1)} %shard_map.64) | data formatting | bytes 16384
